TPU v7x, 32 devices: a whole 2x2x4 slice. The times are simulated.
32 devices in a mesh: dp: 8 (over z, y), tensor: 4 (over x, core).
Axes of the slice: x: 2, y: 2, z: 4, core: 2. Of those that a mesh axis runs over, the one named last changes fastest.
Arguments:
- tokens: bfloat16 [8192, 768], P(('dp', 'tensor')), may hold values from -6 to 6
- cotangent: bfloat16 [8192, 768], P(('dp', 'tensor')), may hold values from -6 to 6
- segments: int32 [8192], P('dp'), may hold values from 0 to 95, as said below
- lengths: int32 [32, 2], P('dp'), may hold values from 2 to 197, as said below
- rel_index: int32 [8192, 256], P('dp'), may hold values from 0 to 731, as said below
- w_qkv: bfloat16 [2, 768, 3, 768], P(None, None, None, 'tensor'), may hold values from -0.21875 to 0.21875
- qv_bias: bfloat16 [2, 2, 768], P(None, None, 'tensor'), may hold values from -3 to 3
- w_out: bfloat16 [2, 768, 768], P(None, 'tensor'), may hold values from -0.875 to 0.875
- w_fc1: bfloat16 [2, 768, 3072], P(None, None, 'tensor'), may hold values from -0.21875 to 0.21875
- fc1_bias: bfloat16 [2, 3072], P(None, 'tensor'), may hold values from -3 to 3
- w_fc2: bfloat16 [2, 3072, 768], P(None, 'tensor'), may hold values from -0.109375 to 0.109375
- rel_table: bfloat16 [2, 732, 12], P(None, None, 'tensor'), may hold values from -5 to 5
- ln_gain: float32 [2, 2, 768], replicated, may hold values from 0.25 to 1.75
- ln_bias: float32 [2, 2, 768], replicated, may hold values from -2 to 2
- layer_scale: float32 [2, 2, 768], replicated, may hold values from 0.25 to 1.75
- row_bias: float32 [2, 2, 768], replicated, may hold values from -2 to 2
Outputs:
- result: bfloat16 [8192, 768], P(('dp', 'tensor'))
- d_tokens: float32 [8192, 768], P(('dp', 'tensor'))
- d_w_qkv: float32 [2, 768, 3, 768], P(None, None, None, 'tensor')
- d_qv_bias: float32 [2, 2, 768], P(None, None, 'tensor')
- d_w_out: float32 [2, 768, 768], P(None, 'tensor')
- d_w_fc1: float32 [2, 768, 3072], P(None, None, 'tensor')
- d_fc1_bias: float32 [2, 3072], P(None, 'tensor')
- d_w_fc2: float32 [2, 3072, 768], P(None, 'tensor')
- d_rel_table: float32 [2, 732, 12], P(None, None, 'tensor')
- d_ln_gain: float32 [2, 2, 768], replicated
- d_ln_bias: float32 [2, 2, 768], replicated
- d_layer_scale: float32 [2, 2, 768], replicated
- d_row_bias: float32 [2, 2, 768], replicated
Inputs may be any that keep to these rules, and one draw needn't show every extreme that they name: `segments`: rows with equal ids belong to one image, or to the padding that ends one bin of 256 rows. Bin b holds rows of id 3 b (its first image), then 3 b + 1 (its second image), then one or more rows of id 3 b + 2 (padding). `lengths`: the rows of a bin's first and second image, in the order of segments; an image of r by c patches has r c + 1 rows, its class token first, then its patches row by row; a bin's two lengths sum to 255 or less. `rel_index`: for rows i and j of one image: (dr + 13) * 27 + dc + 13 for two patches whose row and column offsets are dr and dc, 729 from the class token to a patch, 730 from a patch to the class token, 731 for the class token with itself. Other entries are arbitrary.
All inputs are finite; a program needn't handle non-finite values.
Results may differ from a plain program's by a relative error of at most 0.023.
Values may be sent and summed in bfloat16 or wider, within the bound.
A program may use at most 128 MiB of HBM per device.

v0:
```python
import math
import jax
import jax.numpy as jnp
from jax import lax
from jax.sharding import PartitionSpec as P

HEAD_DIM = 64


def norm_rows(stream, norm_gain, norm_shift):
    center = stream - jnp.mean(stream, -1, keepdims=True)
    inverse = lax.rsqrt(jnp.mean(center * center, -1, keepdims=True) + 1e-06)
    normal = center * inverse
    return (normal * norm_gain + norm_shift, normal, inverse)


def norm_back(gradient, normal, inverse, norm_gain):
    scaled = gradient * norm_gain
    centered = (
        scaled
        - jnp.mean(scaled, -1, keepdims=True)
        - normal * jnp.mean(scaled * normal, -1, keepdims=True)
    )
    return (inverse * centered, jnp.sum(gradient * normal, 0), jnp.sum(gradient, 0))


def gelu_slope(values):
    return (
        0.5 * (1.0 + lax.erf(values * 0.7071067811865476))
        + values * jnp.exp(-0.5 * values * values) * 0.3989422804014327
    )


def contract_rows(left_side, right_side):
    return lax.dot_general(
        left_side, right_side, (((0,), (0,)), ((), ())), preferred_element_type=jnp.float32
    )


def times_transposed(left_side, right_side):
    return lax.dot_general(
        left_side, right_side, (((1,), (1,)), ((), ())), preferred_element_type=jnp.float32
    )


def block_rows(amount, bin_rows):
    return math.gcd(amount, max(1, 16384 // bin_rows))


def look_up(index_rows, table_used):
    amount, bin_rows = index_rows.shape
    layer_count, entries, head_count = table_used.shape
    step_rows = block_rows(amount, bin_rows)
    index_blocks = index_rows.reshape(amount // step_rows, step_rows * bin_rows)
    columns = jnp.transpose(table_used, (0, 2, 1)).reshape(layer_count * head_count, entries)
    table_rows = lax.broadcasted_iota(jnp.int32, (entries, 1), 0)

    def one_block(index_flat):
        onehot = (table_rows == index_flat[None, :]).astype(jnp.bfloat16)
        return jnp.dot(columns, onehot, preferred_element_type=jnp.float32).astype(jnp.bfloat16)

    looked = lax.map(one_block, index_blocks)
    looked = jnp.transpose(looked, (1, 0, 2)).reshape(
        layer_count, head_count, amount // bin_rows, bin_rows, bin_rows
    )
    return jnp.transpose(looked, (0, 2, 1, 3, 4))


def table_grad(index_rows, score_grads, entries):
    amount, bin_rows = index_rows.shape
    layer_count, bin_total, head_count = (
        score_grads.shape[0],
        score_grads.shape[1],
        score_grads.shape[2],
    )
    step_rows = block_rows(amount, bin_rows)
    step_count = amount // step_rows
    index_blocks = index_rows.reshape(step_count, step_rows * bin_rows)
    pieces = jnp.transpose(score_grads, (0, 2, 1, 3, 4)).reshape(
        layer_count * head_count, step_count, step_rows * bin_rows
    )
    pieces = jnp.transpose(pieces, (1, 0, 2))
    table_rows = lax.broadcasted_iota(jnp.int32, (entries, 1), 0)

    def add_block(totals, element):
        onehot = (table_rows == element[0][None, :]).astype(jnp.bfloat16)
        return (totals + times_transposed(element[1], onehot), None)

    totals, unused_out = lax.scan(
        add_block,
        jnp.zeros((layer_count * head_count, entries), jnp.float32),
        (index_blocks, pieces),
    )
    return jnp.transpose(totals.reshape(layer_count, head_count, entries), (0, 2, 1))


def attend_scores(queries, key_rows, position_bias, same_image, head_count, score_scale):
    local_width = queries.shape[1]
    blocked = (same_image.shape[0], same_image.shape[1], head_count, local_width // head_count)
    products = jnp.einsum(
        "bqhd,bkhd->bhqk",
        queries.reshape(blocked),
        key_rows.reshape(blocked),
        preferred_element_type=jnp.float32,
    )
    return jnp.where(
        same_image[:, None],
        products * score_scale + position_bias.astype(jnp.float32),
        -1000000000.0,
    )


def attend(queries, key_rows, values, position_bias, same_image, head_count, score_scale):
    scores = attend_scores(queries, key_rows, position_bias, same_image, head_count, score_scale)
    highest = jnp.max(scores, -1, keepdims=True)
    powers = jnp.exp(scores - highest)
    totals = jnp.sum(powers, -1, keepdims=True)
    weights = (powers / totals).astype(jnp.bfloat16)
    local_width = queries.shape[1]
    blocked = (same_image.shape[0], same_image.shape[1], head_count, local_width // head_count)
    mixture = jnp.einsum(
        "bhqk,bkhd->bqhd", weights, values.reshape(blocked), preferred_element_type=jnp.float32
    )
    return (mixture.reshape(queries.shape).astype(jnp.bfloat16), highest + jnp.log(totals))


def attend_back(
    queries,
    key_rows,
    values,
    position_bias,
    same_image,
    log_totals,
    grad_mix,
    head_count,
    score_scale,
):
    scores = attend_scores(queries, key_rows, position_bias, same_image, head_count, score_scale)
    weights = jnp.exp(scores - log_totals)
    local_width = queries.shape[1]
    blocked = (same_image.shape[0], same_image.shape[1], head_count, local_width // head_count)
    grad_blocked = grad_mix.reshape(blocked)
    grad_weights = jnp.einsum(
        "bqhd,bkhd->bhqk", grad_blocked, values.reshape(blocked), preferred_element_type=jnp.float32
    )
    grad_values = jnp.einsum(
        "bhqk,bqhd->bkhd",
        weights.astype(jnp.bfloat16),
        grad_blocked,
        preferred_element_type=jnp.float32,
    )
    centered = jnp.sum(weights * grad_weights, -1, keepdims=True)
    grad_scores = (weights * (grad_weights - centered)).astype(jnp.bfloat16)
    grad_query = (
        jnp.einsum(
            "bhqk,bkhd->bqhd",
            grad_scores,
            key_rows.reshape(blocked),
            preferred_element_type=jnp.float32,
        )
        * score_scale
    )
    grad_key = (
        jnp.einsum(
            "bhqk,bqhd->bkhd",
            grad_scores,
            queries.reshape(blocked),
            preferred_element_type=jnp.float32,
        )
        * score_scale
    )
    flat_shape = queries.shape
    return (
        grad_query.reshape(flat_shape).astype(jnp.bfloat16),
        grad_key.reshape(flat_shape).astype(jnp.bfloat16),
        grad_values.reshape(flat_shape).astype(jnp.bfloat16),
        grad_scores,
    )


def per_device(
    tokens,
    cotangent,
    segments,
    lengths,
    rel_index,
    w_qkv,
    qv_bias,
    w_out,
    w_fc1,
    fc1_bias,
    w_fc2,
    rel_table,
    ln_gain,
    ln_bias,
    layer_scale,
    row_bias,
):
    own_rows, width = tokens.shape
    group_rows, bin_rows = rel_index.shape
    layer_count = w_qkv.shape[0]
    entries = rel_table.shape[1]
    place = lax.axis_index("tensor")
    score_scale = float(HEAD_DIM) ** (-0.5)
    totals = jnp.sum(lengths, 1)
    inside = jnp.arange(group_rows) % bin_rows < jnp.repeat(totals, bin_rows)
    valid = lax.dynamic_slice_in_dim(inside, place * own_rows, own_rows)[:, None]
    proj_qkv, proj_bias, proj_out, proj_up, up_bias, proj_down, table_used = (
        w_qkv,
        qv_bias,
        w_out,
        w_fc1,
        fc1_bias,
        w_fc2,
        rel_table,
    )
    head_count = table_used.shape[2]
    local_width = proj_qkv.shape[3]
    bin_total = rel_index.shape[0] // bin_rows
    seg_bins = segments.reshape(bin_total, bin_rows)
    same_image = seg_bins[:, :, None] == seg_bins[:, None, :]
    position_bias = look_up(rel_index, table_used)

    def spread_rows(values):
        return lax.all_gather(values, "tensor", axis=0, tiled=True)

    def spread_grads(values):
        return lax.all_gather(values, "tensor", axis=0, tiled=True)

    def project_rows(left_side, right_side):
        return lax.psum_scatter(
            jnp.dot(left_side, right_side, preferred_element_type=jnp.float32).astype(jnp.bfloat16),
            "tensor",
            scatter_dimension=0,
            tiled=True,
        ).astype(jnp.float32)

    def project_grads(left_side, right_side):
        return lax.psum_scatter(
            times_transposed(left_side, right_side).astype(jnp.bfloat16),
            "tensor",
            scatter_dimension=0,
            tiled=True,
        ).astype(jnp.float32)

    stream = tokens.astype(jnp.float32)
    kept_state = []
    for layer_at in range(layer_count):
        layer_qkv = proj_qkv[layer_at].reshape(width, 3 * local_width)
        normed, normal_a, inverse_a = norm_rows(stream, ln_gain[layer_at, 0], ln_bias[layer_at, 0])
        spread_a = spread_rows(normed.astype(jnp.bfloat16))
        mixed_proj = jnp.dot(spread_a, layer_qkv, preferred_element_type=jnp.float32).reshape(
            -1, 3, local_width
        )
        biases = proj_bias[layer_at].astype(jnp.float32)
        queries = (mixed_proj[:, 0] + biases[0]).astype(jnp.bfloat16)
        key_rows = mixed_proj[:, 1].astype(jnp.bfloat16)
        values = (mixed_proj[:, 2] + biases[1]).astype(jnp.bfloat16)
        mixture, log_totals = attend(
            queries, key_rows, values, position_bias[layer_at], same_image, head_count, score_scale
        )
        branch_a = project_rows(mixture, proj_out[layer_at]) + row_bias[layer_at, 0]
        middle = stream + layer_scale[layer_at, 0] * branch_a
        normed_b, normal_b, inverse_b = norm_rows(
            middle, ln_gain[layer_at, 1], ln_bias[layer_at, 1]
        )
        spread_b = spread_rows(normed_b.astype(jnp.bfloat16))
        hidden = jnp.dot(spread_b, proj_up[layer_at], preferred_element_type=jnp.float32) + up_bias[
            layer_at
        ].astype(jnp.float32)
        active = jax.nn.gelu(hidden, approximate=False).astype(jnp.bfloat16)
        branch_b = project_rows(active, proj_down[layer_at]) + row_bias[layer_at, 1]
        kept_state.append(
            (
                normal_a,
                inverse_a,
                spread_a,
                queries,
                key_rows,
                values,
                mixture,
                log_totals,
                branch_a,
                normal_b,
                inverse_b,
                spread_b,
                hidden,
                active,
                branch_b,
            )
        )
        stream = middle + layer_scale[layer_at, 1] * branch_b
    result = jnp.where(valid, stream, 0.0).astype(jnp.bfloat16)
    gradient = jnp.where(valid, cotangent.astype(jnp.float32), 0.0)
    list_qkv = [None] * layer_count
    list_qvb = [None] * layer_count
    list_out = [None] * layer_count
    list_up = [None] * layer_count
    list_upb = [None] * layer_count
    list_down = [None] * layer_count
    list_scores = [None] * layer_count
    list_gain = [None] * layer_count
    list_shift = [None] * layer_count
    list_scale = [None] * layer_count
    list_rowb = [None] * layer_count
    for layer_at in reversed(range(layer_count)):
        (
            normal_a,
            inverse_a,
            spread_a,
            queries,
            key_rows,
            values,
            mixture,
            log_totals,
            branch_a,
            normal_b,
            inverse_b,
            spread_b,
            hidden,
            active,
            branch_b,
        ) = kept_state[layer_at]
        scale_b = jnp.sum(gradient * branch_b, 0)
        rowb_b = layer_scale[layer_at, 1] * jnp.sum(gradient, 0)
        spread_down = spread_grads((gradient * layer_scale[layer_at, 1]).astype(jnp.bfloat16))
        list_down[layer_at] = contract_rows(active, spread_down)
        grad_active = times_transposed(spread_down, proj_down[layer_at])
        grad_hidden = (grad_active * gelu_slope(hidden)).astype(jnp.bfloat16)
        list_upb[layer_at] = jnp.sum(grad_hidden.astype(jnp.float32), 0)
        list_up[layer_at] = contract_rows(spread_b, grad_hidden)
        back_b, gain_b, shift_b = norm_back(
            project_grads(grad_hidden, proj_up[layer_at]), normal_b, inverse_b, ln_gain[layer_at, 1]
        )
        gradient = gradient + back_b
        scale_a = jnp.sum(gradient * branch_a, 0)
        rowb_a = layer_scale[layer_at, 0] * jnp.sum(gradient, 0)
        spread_attn = spread_grads((gradient * layer_scale[layer_at, 0]).astype(jnp.bfloat16))
        list_out[layer_at] = contract_rows(mixture, spread_attn)
        grad_mix = times_transposed(spread_attn, proj_out[layer_at]).astype(jnp.bfloat16)
        grad_query, grad_key, grad_value, grad_scores = attend_back(
            queries,
            key_rows,
            values,
            position_bias[layer_at],
            same_image,
            log_totals,
            grad_mix,
            head_count,
            score_scale,
        )
        list_scores[layer_at] = grad_scores
        list_qvb[layer_at] = jnp.stack(
            [jnp.sum(grad_query.astype(jnp.float32), 0), jnp.sum(grad_value.astype(jnp.float32), 0)]
        )
        grad_proj = jnp.stack([grad_query, grad_key, grad_value], 1).reshape(-1, 3 * local_width)
        list_qkv[layer_at] = contract_rows(spread_a, grad_proj).reshape(width, 3, local_width)
        back_a, gain_a, shift_a = norm_back(
            project_grads(grad_proj, proj_qkv[layer_at].reshape(width, 3 * local_width)),
            normal_a,
            inverse_a,
            ln_gain[layer_at, 0],
        )
        gradient = gradient + back_a
        list_gain[layer_at] = jnp.stack([gain_a, gain_b])
        list_shift[layer_at] = jnp.stack([shift_a, shift_b])
        list_scale[layer_at] = jnp.stack([scale_a, scale_b])
        list_rowb[layer_at] = jnp.stack([rowb_a, rowb_b])
    qkv_all = jnp.stack(list_qkv)
    qvb_all = jnp.stack(list_qvb)
    out_all = jnp.stack(list_out)
    up_all = jnp.stack(list_up)
    upb_all = jnp.stack(list_upb)
    down_all = jnp.stack(list_down)
    table_all = table_grad(rel_index, jnp.stack(list_scores), entries)
    qkv_all, qvb_all, out_all, up_all, upb_all, down_all, table_all = lax.psum(
        (qkv_all, qvb_all, out_all, up_all, upb_all, down_all, table_all), "dp"
    )
    gain_all, shift_all, scale_all, rowb_all = lax.psum(
        (jnp.stack(list_gain), jnp.stack(list_shift), jnp.stack(list_scale), jnp.stack(list_rowb)),
        ("dp", "tensor"),
    )
    return (
        result,
        gradient,
        qkv_all,
        qvb_all,
        out_all,
        up_all,
        upb_all,
        down_all,
        table_all,
        gain_all,
        shift_all,
        scale_all,
        rowb_all,
    )


def solution(mesh):
    in_specs = (
        P(("dp", "tensor"), None),
        P(("dp", "tensor"), None),
        P("dp"),
        P("dp", None),
        P("dp", None),
        P(None, None, None, "tensor"),
        P(None, None, "tensor"),
        P(None, "tensor", None),
        P(None, None, "tensor"),
        P(None, "tensor"),
        P(None, "tensor", None),
        P(None, None, "tensor"),
        P(),
        P(),
        P(),
        P(),
    )
    out_specs = (
        P(("dp", "tensor"), None),
        P(("dp", "tensor"), None),
        P(None, None, None, "tensor"),
        P(None, None, "tensor"),
        P(None, "tensor", None),
        P(None, None, "tensor"),
        P(None, "tensor"),
        P(None, "tensor", None),
        P(None, None, "tensor"),
        P(),
        P(),
        P(),
        P(),
    )
    return jax.shard_map(
        per_device, mesh=mesh, in_specs=in_specs, out_specs=out_specs, check_vma=False
    )
```

profile of v0, /device:TPU:0, one launch (start us, length us, event | category | flops | bytes accessed | tf_op | source)
XLA Modules:
  0.0 1150.7 jit_solution(10076995145062278454)
XLA Ops:
  15.4 128.6 %while.22 = (s32[]{:T(128)}, bf16[16,6,16384]{2,1,0:T(8,128)(2,1)}, s32[16,16384]{1,0:T(8,128)S(1)}, bf16[6,732]{1,0:T(8,128)(2,1)S(1)}, s32[]{:T(128)}) while((s32[]{:T(128)}, bf16[16,6,16384]{2,1,0:T(8,128)(2,1)}, s32[16,16384]{1,0:T(8,128)S(1)}, bf16[6,732]{1,0:T(8,128)(2,1)S(1)}, s32[]{:T(128)}) %tuple.112), condition=%wide.region_4.5_spmd.clone, body=%wide.region_3.4_spmd.clone.sunk | while | flops 156008448 | bytes 467613 | solution.py:62
  174.2 29.5 %reduce-scatter.9.cloned.1.call-done = bf16[256,768]{1,0:T(8,128)(2,1)} async-done(((bf16[1024,768]{1,0:T(8,128)(2,1)}), bf16[256,768]{1,0:T(8,128)(2,1)}) %reduce-scatter.9.cloned.1.call-update) | async-done | bytes 393232 | tf_op jit(solution)/shard_map/reduce_scatter | solution.py:231
  210.2 18.4 %all-gather.11.cloned.1.call-done = bf16[1024,768]{1,0:T(8,128)(2,1)} async-done(((bf16[256,768]{1,0:T(8,128)(2,1)}), bf16[1024,768]{1,0:T(8,128)(2,1)}) %all-gather.11.cloned.1.call-update) | async-done | bytes 1572880 | tf_op jit(solution)/shard_map/all_gather | solution.py:225
  228.6 11.0 fusion.17
  243.3 28.3 %reduce-scatter.11.cloned.1.call-done = bf16[256,768]{1,0:T(8,128)(2,1)} async-done(((bf16[1024,768]{1,0:T(8,128)(2,1)}), bf16[256,768]{1,0:T(8,128)(2,1)}) %reduce-scatter.11.cloned.1.call-update) | async-done | bytes 393232 | tf_op jit(solution)/shard_map/reduce_scatter | solution.py:231
  275.6 11.0 reduce-scatter.13.cloned.1.call-start
  315.4 28.3 %reduce-scatter.13.cloned.1.call-done = bf16[256,768]{1,0:T(8,128)(2,1)} async-done(((bf16[1024,768]{1,0:T(8,128)(2,1)}), bf16[256,768]{1,0:T(8,128)(2,1)}) %reduce-scatter.13.cloned.1.call-update) | async-done | bytes 393232 | tf_op jit(solution)/shard_map/reduce_scatter | solution.py:231
  351.1 16.4 %all-gather.15.cloned.1.call-done = bf16[1024,768]{1,0:T(8,128)(2,1)} async-done(((bf16[256,768]{1,0:T(8,128)(2,1)}), bf16[1024,768]{1,0:T(8,128)(2,1)}) %all-gather.15.cloned.1.call-update) | async-done | bytes 1572880 | tf_op jit(solution)/shard_map/all_gather | solution.py:225
  367.5 11.2 fusion.20
  378.7 10.2 all-gather.17.cloned.1.call-done
  402.7 23.9 %reduce-scatter.17.cloned.1.call-done = bf16[256,768]{1,0:T(8,128)(2,1)} async-done(((bf16[1024,768]{1,0:T(8,128)(2,1)}), bf16[256,768]{1,0:T(8,128)(2,1)}) %reduce-scatter.17.cloned.1.call-update) | async-done | bytes 393232 | tf_op jit(solution)/shard_map/reduce_scatter | solution.py:239
  430.0 27.2 %reduce-scatter.15.cloned.1.call-done = bf16[256,768]{1,0:T(8,128)(2,1)} async-done(((bf16[1024,768]{1,0:T(8,128)(2,1)}), bf16[256,768]{1,0:T(8,128)(2,1)}) %reduce-scatter.15.cloned.1.call-update) | async-done | bytes 393232 | tf_op jit(solution)/shard_map/reduce_scatter | solution.py:231
  466.4 15.9 %all-gather.19.cloned.1.call-done = bf16[1024,768]{1,0:T(8,128)(2,1)} async-done(((bf16[256,768]{1,0:T(8,128)(2,1)}), bf16[1024,768]{1,0:T(8,128)(2,1)}) %all-gather.19.cloned.1.call-update) | async-done | bytes 1572880 | tf_op jit(solution)/shard_map/all_gather | solution.py:228
  516.0 28.3 %reduce-scatter.19.cloned.1.call-done = bf16[256,768]{1,0:T(8,128)(2,1)} async-done(((bf16[1024,768]{1,0:T(8,128)(2,1)}), bf16[256,768]{1,0:T(8,128)(2,1)}) %reduce-scatter.19.cloned.1.call-update) | async-done | bytes 393232 | tf_op jit(solution)/shard_map/reduce_scatter | solution.py:239
  550.9 19.8 %all-gather.21.cloned.1.call-done = bf16[1024,768]{1,0:T(8,128)(2,1)} async-done(((bf16[256,768]{1,0:T(8,128)(2,1)}), bf16[1024,768]{1,0:T(8,128)(2,1)}) %all-gather.21.cloned.1.call-update) | async-done | bytes 1572880 | tf_op jit(solution)/shard_map/all_gather | solution.py:228
  580.1 28.3 %reduce-scatter.21.cloned.1.call-done = bf16[256,768]{1,0:T(8,128)(2,1)} async-done(((bf16[1024,768]{1,0:T(8,128)(2,1)}), bf16[256,768]{1,0:T(8,128)(2,1)}) %reduce-scatter.21.cloned.1.call-update) | async-done | bytes 393232 | tf_op jit(solution)/shard_map/reduce_scatter | solution.py:239
  690.2 169.5 %while.23 = (s32[]{:T(128)}, f32[6,732]{1,0:T(8,128)S(1)}, bf16[16,6,16384]{2,1,0:T(8,128)(2,1)}, s32[16,16384]{1,0:T(8,128)}, s32[]{:T(128)}, /*index=5*/s32[]{:T(128)}) while((s32[]{:T(128)}, f32[6,732]{1,0:T(8,128)S(1)}, bf16[16,6,16384]{2,1,0:T(8,128)(2,1)}, s32[16,16384]{1,0:T(8,128)}, s32[]{:T(128)}, ...), condition=%wide.region_46.47_spmd.clone, body=%wide.region_45.46_spmd.clone.sunk | while | flops 155918912 | bytes 493983 | solution.py:89
  691.5 9.5 fusion.243
  702.1 9.5 fusion.243
  712.7 9.5 fusion.243
  723.3 9.5 fusion.243
  733.8 9.5 fusion.243
  744.4 9.5 fusion.243
  755.0 9.5 fusion.243
  776.1 9.5 fusion.243
  797.3 9.5 fusion.243
  818.4 9.5 fusion.243
  839.6 9.5 fusion.243
  850.2 9.5 fusion.243
  859.9 40.7 %all-reduce.1 = (f32[2,2,192]{2,1,0:T(2,128)}, f32[2,768]{1,0:T(2,128)}, f32[2,732,3]{1,2,0:T(4,128)S(1)}) all-reduce(f32[2,2,192]{2,1,0:T(2,128)S(1)} %pad_maximum_fusion.9, f32[2,768]{1,0:T(2,128)S(1)} %copy-done.67, f32[2,732,3]{1,2,0:T(4,128)S(1)} %bitcast.278), channel_id=1, replica_groups=mesh['dp'=8,'tensor'=4] {'dp'}, use_global_device_ids=true, to_apply=%region_38.39 | all-reduce | flops 6696 | bytes 53568 | tf_op jit(solution)/shard_map/psum | solution.py:376
  902.8 40.4 %all-reduce = (f32[2,2,768]{2,1,0:T(2,128)}, f32[2,2,768]{2,1,0:T(2,128)}, f32[2,2,768]{2,1,0:T(2,128)}, f32[2,2,768]{2,1,0:T(2,128)}) all-reduce(f32[2,2,768]{2,1,0:T(2,128)S(1)} %pad_maximum_fusion.4, f32[2,2,768]{2,1,0:T(2,128)S(1)} %pad_maximum_fusion.5, ...), channel_id=1, replica_groups=mesh['dp'=8,'tensor'=4] {'dp','tensor'}, use_global_device_ids=true, to_apply=%region_52.53 | all-reduce | flops 12288 | bytes 98304 | tf_op jit(solution)/shard_map/psum | solution.py:379
  945.4 187.2 %all-reduce.5.cloned.1.call-done = (f32[2,768,3,192]{1,3,2,0:T(8,128)}, f32[2,192,768]{2,1,0:T(8,128)}, f32[2,768,768]{2,1,0:T(8,128)}, f32[2,768,768]{2,1,0:T(8,128)}) async-done(((f32[2,768,3,192]{1,3,2,0:T(8,128)}, f32[2,192,768]{2,1,0:T(8,128)}, f32[2,768,768]{2,1,0:T(8,128)}, f32[2,768,768]{2,1,0:T(8,128)}), (f32[2,768,3,192]{1,3,2,0:T(8,128)}, f32[2,192,768]{2,1,0:T(8,128)}, f32[2,768,768]{2,1,0:T(8,128)}, ...) | async-done | bytes 14155792 | tf_op jit(solution)/shard_map/psum | solution.py:376
  (519 shorter events, 445.1 us)
Async XLA Ops:
  7.2 340.6 %copy-start = (s32[4,2]{0,1:T(2,128)S(1)}, s32[4,2]{0,1:T(2,128)}, u32[]{:S(2)}) copy-start(s32[4,2]{0,1:T(2,128)} %param.23) | copy-start | bytes 100
  7.2 151.4 %all-gather.9.cloned.1.call-start = ((), (), s32[]{:S(2)}) async-start(), calls=%async_computation.8 | async-start | bytes 1966080 | tf_op jit(solution)/shard_map/all_gather | solution.py:225
  13.1 190.5 %reduce-scatter.9.cloned.1.call-start = ((), (), s32[]{:S(2)}) async-start(), calls=%async_computation.9 | async-start | bytes 1966080 | tf_op jit(solution)/shard_map/reduce_scatter | solution.py:231
  15.4 128.6 %copy-start.103 = (bf16[2,2,192]{2,1,0:T(2,128)(2,1)S(1)}, bf16[2,2,192]{2,1,0:T(2,128)(2,1)}, u32[]{:S(2)}) copy-start(bf16[2,2,192]{2,1,0:T(2,128)(2,1)} %param.26) | copy-start | bytes 4612
  172.6 56.0 %all-gather.11.cloned.1.call-start = ((), (), s32[]{:S(2)}) async-start(), calls=%async_computation.10 | async-start | bytes 1966080 | tf_op jit(solution)/shard_map/all_gather | solution.py:225
  208.8 62.8 %reduce-scatter.11.cloned.1.call-start = ((), (), s32[]{:S(2)}) async-start(), calls=%async_computation.11 | async-start | bytes 1966080 | tf_op jit(solution)/shard_map/reduce_scatter | solution.py:231
  243.3 52.2 %all-gather.13.cloned.1.call-start = ((), (), s32[]{:S(2)}) async-start(), calls=%async_computation.12 | async-start | bytes 1966080 | tf_op jit(solution)/shard_map/all_gather | solution.py:225
  275.6 68.1 %reduce-scatter.13.cloned.1.call-start = ((), (), s32[]{:S(2)}) async-start(), calls=%async_computation.13 | async-start | bytes 1966080 | tf_op jit(solution)/shard_map/reduce_scatter | solution.py:231
  315.4 52.1 %all-gather.15.cloned.1.call-start = ((), (), s32[]{:S(2)}) async-start(), calls=%async_computation.14 | async-start | bytes 1966080 | tf_op jit(solution)/shard_map/all_gather | solution.py:225
  347.7 41.2 %all-gather.17.cloned.1.call-start = ((), (), s32[]{:S(2)}) async-start(), calls=%async_computation.16 | async-start | bytes 1966080 | tf_op jit(solution)/shard_map/all_gather | solution.py:228
  351.1 75.5 %reduce-scatter.17.cloned.1.call-start = ((), (), s32[]{:S(2)}) async-start(), calls=%async_computation.17 | async-start | bytes 1966080 | tf_op jit(solution)/shard_map/reduce_scatter | solution.py:239
  398.3 58.9 %reduce-scatter.15.cloned.1.call-start = ((), (), s32[]{:S(2)}) async-start(), calls=%async_computation.15 | async-start | bytes 1966080 | tf_op jit(solution)/shard_map/reduce_scatter | solution.py:231
  402.6 79.7 %all-gather.19.cloned.1.call-start = ((), (), s32[]{:S(2)}) async-start(), calls=%async_computation.18 | async-start | bytes 1966080 | tf_op jit(solution)/shard_map/all_gather | solution.py:228
  462.6 81.7 %reduce-scatter.19.cloned.1.call-start = ((), (), s32[]{:S(2)}) async-start(), calls=%async_computation.19 | async-start | bytes 1966080 | tf_op jit(solution)/shard_map/reduce_scatter | solution.py:239
  515.9 54.8 %all-gather.21.cloned.1.call-start = ((), (), s32[]{:S(2)}) async-start(), calls=%async_computation.20 | async-start | bytes 1966080 | tf_op jit(solution)/shard_map/all_gather | solution.py:228
  550.9 57.5 %reduce-scatter.21.cloned.1.call-start = ((), (), s32[]{:S(2)}) async-start(), calls=%async_computation.21 | async-start | bytes 1966080 | tf_op jit(solution)/shard_map/reduce_scatter | solution.py:239
  580.0 56.3 %all-gather.23.cloned.1.call-start = ((), (), s32[]{:S(2)}) async-start(), calls=%async_computation.22 | async-start | bytes 1966080 | tf_op jit(solution)/shard_map/all_gather | solution.py:228
  614.8 286.4 %reduce-scatter.23.cloned.1.call-start = ((), (), s32[]{:S(2)}) async-start(), calls=%async_computation.23 | async-start | bytes 1966080 | tf_op jit(solution)/shard_map/reduce_scatter | solution.py:239
  654.3 478.3 %all-reduce.5.cloned.1.call-start = ((), (), s32[]{:S(2)}) async-start(), calls=%async_computation.24 | async-start | bytes 28311552 | tf_op jit(solution)/shard_map/psum | solution.py:376
  690.1 169.6 %copy-start.90 = (f32[3,64]{1,0:T(4,128)S(1)}, f32[3,64]{1,0:T(4,128)}, u32[]{:S(2)}) copy-start(f32[3,64]{1,0:T(4,128)} %get-tuple-element.224) | copy-start | bytes 2308
  690.1 169.6 %copy-start.95 = (f32[3,64]{1,0:T(4,128)S(1)}, f32[3,64]{1,0:T(4,128)}, u32[]{:S(2)}) copy-start(f32[3,64]{1,0:T(4,128)} %get-tuple-element.226) | copy-start | bytes 2308
  690.1 169.8 %copy-start.94 = (f32[1,2,192]{2,1,0:T(2,128)S(1)}, f32[1,2,192]{2,1,0:T(2,128)}, u32[]{:S(2)}) copy-start(f32[1,2,192]{2,1,0:T(2,128)} %maximum_bitcast_fusion.10) | copy-start | bytes 4612
  690.1 169.8 %copy-start.67 = (f32[2,768]{1,0:T(2,128)S(1)}, f32[2,768]{1,0:T(2,128)}, u32[]{:S(2)}) copy-start(f32[2,768]{1,0:T(2,128)} %pad_maximum_fusion.8) | copy-start | bytes 18436
  690.1 211.1 %copy-start.44 = (f32[768]{0:T(1024)S(1)}, f32[768]{0:T(1024)}, u32[]{:S(2)}) copy-start(f32[768]{0:T(1024)} %copy-done.43) | copy-start | bytes 9220
  690.1 211.1 %copy-start.58 = (f32[256]{0:T(256)S(1)}, f32[256]{0:T(256)}, u32[]{:S(2)}) copy-start(f32[256]{0:T(256)} %copy-done.57) | copy-start | bytes 3076
  690.1 211.1 %copy-start.69 = (f32[256]{0:T(256)S(1)}, f32[256]{0:T(256)}, u32[]{:S(2)}) copy-start(f32[256]{0:T(256)} %copy-done.68) | copy-start | bytes 3076
  690.1 212.6 %copy-start.87 = (f32[1,768]{1,0:T(1,128)S(1)}, f32[1,768]{1,0:T(1,128)}, u32[]{:S(2)}) copy-start(f32[1,768]{1,0:T(1,128)} %stack.215) | copy-start | bytes 9220
  690.1 212.6 %copy-start.88 = (f32[1,768]{1,0:T(1,128)S(1)}, f32[1,768]{1,0:T(1,128)}, u32[]{:S(2)}) copy-start(f32[1,768]{1,0:T(1,128)} %stack.224) | copy-start | bytes 9220
  690.1 212.6 %copy-start.64 = (f32[1,2,768]{2,1,0:T(2,128)S(1)}, f32[1,2,768]{2,1,0:T(2,128)}, u32[]{:S(2)}) copy-start(f32[1,2,768]{2,1,0:T(2,128)} %maximum_bitcast_fusion.2) | copy-start | bytes 18436
  690.1 212.6 %copy-start.65 = (f32[1,2,768]{2,1,0:T(2,128)S(1)}, f32[1,2,768]{2,1,0:T(2,128)}, u32[]{:S(2)}) copy-start(f32[1,2,768]{2,1,0:T(2,128)} %maximum_bitcast_fusion.4) | copy-start | bytes 18436
  690.2 212.6 %copy-start.54 = (f32[2,2,768]{2,1,0:T(2,128)S(1)}, f32[2,2,768]{2,1,0:T(2,128)}, u32[]{:S(2)}) copy-start(f32[2,2,768]{2,1,0:T(2,128)} %pad_maximum_fusion.7) | copy-start | bytes 36868
  690.2 253.1 %copy-start.12 = (f32[256,768]{1,0:T(8,128)S(1)}, f32[256,768]{1,0:T(8,128)}, u32[]{:S(2)}) copy-start(f32[256,768]{1,0:T(8,128)} %copy-done.11) | copy-start | bytes 2359300
  (105 other events, 614.8 us)
Sparse Core Ops, SparseCore 0:
  13.3 22.3 all-gather.8
  172.7 30.8 reduce-scatter.8
  208.9 19.6 all-gather.10
  243.4 28.1 reduce-scatter.10
  275.8 19.6 all-gather.12
  315.5 28.1 reduce-scatter.12
  347.8 19.6 all-gather.14
  369.2 19.7 all-gather.16
  398.4 28.1 reduce-scatter.16
  429.0 28.1 reduce-scatter.14
  462.7 19.6 all-gather.18
  516.0 28.1 reduce-scatter.18
  551.0 19.6 all-gather.20
  580.1 28.1 reduce-scatter.20
  614.9 19.6 all-gather.22
  654.4 28.1 reduce-scatter.22
  689.5 443.0 all-reduce.4
where the time goes:
time: 1160 us; the launch traced here: 1150 us
  waiting for transfers between devices  468 us (40%)
  matrix products  388 us (33%)
  local copies, waits for them, and re-layouts  124 us (11%)
  blocking collectives  81.1 us (7%)
  other arithmetic  61.5 us (5%)
  between operations  15.7 us (1%)
  starting transfers between devices  12.5 us (1%)
    psum x1, waiting for transfers between devices, per_device(): lax.psum((qkv_all, qvb_all, out_all, up_all, upb_all, down_all, table_all...  187 us
    dot_general x24, matrix products, times_transposed(): lax.dot_general(left_side, right_side, (((1,), (1,)), ((), ())), preferre...  180 us
    dot_general x16, matrix products, one_block(): jnp.dot(columns, onehot, preferred_element_type=jnp.float32)  128 us
    reduce_scatter x4, waiting for transfers between devices, project_rows(): lax.psum_scatter(jnp.dot(left_side, right_side, preferred_element_type=jn...  113 us
    reduce_scatter x4, waiting for transfers between devices, project_grads(): lax.psum_scatter(times_transposed(left_side, right_side).astype(jnp.bfloa...  80.5 us
    all_gather x4, waiting for transfers between devices, spread_grads(): return lax.all_gather(values, 'tensor', axis=0, tiled=True)  45.9 us
    all_gather x4, waiting for transfers between devices, spread_rows(): return lax.all_gather(values, 'tensor', axis=0, tiled=True)  40.9 us
    psum x1, blocking collectives, per_device(): lax.psum((qkv_all, qvb_all, out_all, up_all, upb_all, down_all, table_all...  40.7 us
  transfers between devices with their start and end apart: 17, of which 14 were waited for; matrix products, arithmetic and copies ran while one was open for 35% of the time, Pallas kernels for 0%

commit v1 on v0

--- a/solution.py
+++ b/solution.py
@@ -376,9 +376,12 @@
     qkv_all, qvb_all, out_all, up_all, upb_all, down_all, table_all = lax.psum(
         (qkv_all, qvb_all, out_all, up_all, upb_all, down_all, table_all), "dp"
     )
-    gain_all, shift_all, scale_all, rowb_all = lax.psum(
-        (jnp.stack(list_gain), jnp.stack(list_shift), jnp.stack(list_scale), jnp.stack(list_rowb)),
-        ("dp", "tensor"),
+
+    def find_the_body(frame_in):
+        return jax.lax.psum(jax.lax.psum(frame_in, "tensor"), "dp")
+
+    gain_all, shift_all, scale_all, rowb_all = find_the_body(
+        (jnp.stack(list_gain), jnp.stack(list_shift), jnp.stack(list_scale), jnp.stack(list_rowb))
     )
     return (
         result,

time: 1160 us -> 1420 us (1.22)
  waiting for transfers between devices: 468 us -> 771 us
  blocking collectives: 81.1 us -> 11.2 us
    psum x1 -> x2, waiting for transfers between devices: 187 us -> 512 us  [per_device(): lax.psum((qkv_all, qvb_all, out_all, up_all, upb_all, down_all, table_all...]
    psum x2 -> x1, blocking collectives: 81.1 us -> 11.2 us  [find_the_body(): return jax.lax.psum(jax.lax.psum(frame_in, 'tensor'), 'dp')]
    reduce_scatter x4, waiting for transfers between devices: 80.5 us -> 56.9 us  [project_grads(): lax.psum_scatter(times_transposed(left_side, right_side).astype(jnp.bfloa...]
    unnamed x254 -> x260, local copies, waits for them, and re-layouts: 36.6 us -> 39.4 us
  transfers between devices with their start and end apart: 17 -> 18, of which waited for: 14 -> 16; matrix products, arithmetic and copies ran while one was open for 35% -> 30% of each run, Pallas kernels for 0% -> 0%
where the time goes in v1:
time: 1420 us; the launch traced here: 1410 us
  waiting for transfers between devices  771 us (54%)
  matrix products  400 us (28%)
  local copies, waits for them, and re-layouts  131 us (9%)
  other arithmetic  63.3 us (4%)
  between operations  16 us (1%)
    psum x2, waiting for transfers between devices, per_device(): lax.psum((qkv_all, qvb_all, out_all, up_all, upb_all, down_all, table_all...  512 us
    dot_general x24, matrix products, times_transposed(): lax.dot_general(left_side, right_side, (((1,), (1,)), ((), ())), preferre...  191 us
    dot_general x16, matrix products, one_block(): jnp.dot(columns, onehot, preferred_element_type=jnp.float32)  128 us
    reduce_scatter x4, waiting for transfers between devices, project_rows(): lax.psum_scatter(jnp.dot(left_side, right_side, preferred_element_type=jn...  113 us
    reduce_scatter x4, waiting for transfers between devices, project_grads(): lax.psum_scatter(times_transposed(left_side, right_side).astype(jnp.bfloa...  56.9 us
    all_gather x4, waiting for transfers between devices, spread_grads(): return lax.all_gather(values, 'tensor', axis=0, tiled=True)  47.9 us
    all_gather x4, waiting for transfers between devices, spread_rows(): return lax.all_gather(values, 'tensor', axis=0, tiled=True)  41 us
    unnamed x260, local copies, waits for them, and re-layouts  39.4 us
  transfers between devices with their start and end apart: 18, of which 16 were waited for; matrix products, arithmetic and copies ran while one was open for 30% of the time, Pallas kernels for 0%

profile of v1, /device:TPU:0, one launch (start us, length us, event | category | flops | bytes accessed | tf_op | source)
XLA Modules:
  0.0 1406.7 jit_solution(11211086813413113507)
XLA Ops:
  15.4 128.6 %while.22 = (s32[]{:T(128)}, bf16[16,6,16384]{2,1,0:T(8,128)(2,1)}, s32[16,16384]{1,0:T(8,128)S(1)}, bf16[6,732]{1,0:T(8,128)(2,1)S(1)}, s32[]{:T(128)}) while((s32[]{:T(128)}, bf16[16,6,16384]{2,1,0:T(8,128)(2,1)}, s32[16,16384]{1,0:T(8,128)S(1)}, bf16[6,732]{1,0:T(8,128)(2,1)S(1)}, s32[]{:T(128)}) %tuple.112), condition=%wide.region_4.5_spmd.clone, body=%wide.region_3.4_spmd.clone.sunk | while | flops 156008448 | bytes 467613 | solution.py:62
  174.2 29.5 %reduce-scatter.9.cloned.1.call-done = bf16[256,768]{1,0:T(8,128)(2,1)} async-done(((bf16[1024,768]{1,0:T(8,128)(2,1)}), bf16[256,768]{1,0:T(8,128)(2,1)}) %reduce-scatter.9.cloned.1.call-update) | async-done | bytes 393232 | tf_op jit(solution)/shard_map/reduce_scatter | solution.py:231
  210.2 18.4 %all-gather.11.cloned.1.call-done = bf16[1024,768]{1,0:T(8,128)(2,1)} async-done(((bf16[256,768]{1,0:T(8,128)(2,1)}), bf16[1024,768]{1,0:T(8,128)(2,1)}) %all-gather.11.cloned.1.call-update) | async-done | bytes 1572880 | tf_op jit(solution)/shard_map/all_gather | solution.py:225
  228.7 11.0 fusion.17
  243.4 28.3 %reduce-scatter.11.cloned.1.call-done = bf16[256,768]{1,0:T(8,128)(2,1)} async-done(((bf16[1024,768]{1,0:T(8,128)(2,1)}), bf16[256,768]{1,0:T(8,128)(2,1)}) %reduce-scatter.11.cloned.1.call-update) | async-done | bytes 393232 | tf_op jit(solution)/shard_map/reduce_scatter | solution.py:231
  275.7 11.0 reduce-scatter.13.cloned.1.call-start
  315.5 28.3 %reduce-scatter.13.cloned.1.call-done = bf16[256,768]{1,0:T(8,128)(2,1)} async-done(((bf16[1024,768]{1,0:T(8,128)(2,1)}), bf16[256,768]{1,0:T(8,128)(2,1)}) %reduce-scatter.13.cloned.1.call-update) | async-done | bytes 393232 | tf_op jit(solution)/shard_map/reduce_scatter | solution.py:231
  351.2 16.4 %all-gather.15.cloned.1.call-done = bf16[1024,768]{1,0:T(8,128)(2,1)} async-done(((bf16[256,768]{1,0:T(8,128)(2,1)}), bf16[1024,768]{1,0:T(8,128)(2,1)}) %all-gather.15.cloned.1.call-update) | async-done | bytes 1572880 | tf_op jit(solution)/shard_map/all_gather | solution.py:225
  367.6 11.2 fusion.20
  378.9 10.1 all-gather.17.cloned.1.call-done
  402.7 23.9 %reduce-scatter.17.cloned.1.call-done = bf16[256,768]{1,0:T(8,128)(2,1)} async-done(((bf16[1024,768]{1,0:T(8,128)(2,1)}), bf16[256,768]{1,0:T(8,128)(2,1)}) %reduce-scatter.17.cloned.1.call-update) | async-done | bytes 393232 | tf_op jit(solution)/shard_map/reduce_scatter | solution.py:239
  430.0 27.2 %reduce-scatter.15.cloned.1.call-done = bf16[256,768]{1,0:T(8,128)(2,1)} async-done(((bf16[1024,768]{1,0:T(8,128)(2,1)}), bf16[256,768]{1,0:T(8,128)(2,1)}) %reduce-scatter.15.cloned.1.call-update) | async-done | bytes 393232 | tf_op jit(solution)/shard_map/reduce_scatter | solution.py:231
  466.5 15.9 %all-gather.19.cloned.1.call-done = bf16[1024,768]{1,0:T(8,128)(2,1)} async-done(((bf16[256,768]{1,0:T(8,128)(2,1)}), bf16[1024,768]{1,0:T(8,128)(2,1)}) %all-gather.19.cloned.1.call-update) | async-done | bytes 1572880 | tf_op jit(solution)/shard_map/all_gather | solution.py:228
  516.0 28.3 %reduce-scatter.19.cloned.1.call-done = bf16[256,768]{1,0:T(8,128)(2,1)} async-done(((bf16[1024,768]{1,0:T(8,128)(2,1)}), bf16[256,768]{1,0:T(8,128)(2,1)}) %reduce-scatter.19.cloned.1.call-update) | async-done | bytes 393232 | tf_op jit(solution)/shard_map/reduce_scatter | solution.py:239
  551.0 19.8 %all-gather.21.cloned.1.call-done = bf16[1024,768]{1,0:T(8,128)(2,1)} async-done(((bf16[256,768]{1,0:T(8,128)(2,1)}), bf16[1024,768]{1,0:T(8,128)(2,1)}) %all-gather.21.cloned.1.call-update) | async-done | bytes 1572880 | tf_op jit(solution)/shard_map/all_gather | solution.py:228
  668.3 179.0 %while.23 = (s32[]{:T(128)}, f32[6,732]{1,0:T(8,128)}, bf16[16,6,16384]{2,1,0:T(8,128)(2,1)}, s32[16,16384]{1,0:T(8,128)}, s32[]{:T(128)}, /*index=5*/s32[]{:T(128)}) while((s32[]{:T(128)}, f32[6,732]{1,0:T(8,128)}, bf16[16,6,16384]{2,1,0:T(8,128)(2,1)}, s32[16,16384]{1,0:T(8,128)}, s32[]{:T(128)}, /*index=5*/s32[]{:T(128)}) %tuple.157), condition=%wide.region_46.47_spmd.clone, body=%wide.region_45.46_spmd.clone.sunk | while | flops 155918912 | bytes 500991 | solution.py:89
  669.4 10.1 fusion.243
  680.6 10.1 fusion.243
  691.8 10.1 fusion.243
  703.0 10.1 fusion.243
  714.1 10.1 fusion.243
  725.3 10.1 fusion.243
  736.5 10.1 fusion.243
  747.7 10.1 fusion.243
  758.8 10.1 fusion.243
  770.0 10.1 fusion.243
  781.2 10.1 fusion.243
  792.3 10.1 fusion.243
  803.5 10.1 fusion.243
  856.8 11.2 all-reduce.2
  871.6 68.3 %all-reduce.6.cloned.1.call-done = (f32[2,2,192]{2,1,0:T(2,128)}, f32[2,768]{1,0:T(2,128)}, f32[2,732,3]{1,2,0:T(4,128)}, f32[2,2,768]{2,1,0:T(2,128)}, f32[2,2,...) async-done(((f32[2,2,192]{2,1,0:T(2,128)}, f32[2,768]{1,0:T(2,128)}, f32[2,732,3]{1,2,0:T(4,128)}, f32[2,2,768]{2,1,0:T(2,128)}, f32[2,2,768]{2,1,0:T(2,128)}, ...) | async-done | bytes 75952 | tf_op jit(solution)/shard_map/psum | solution.py:376
  941.3 444.0 %all-reduce.8.cloned.1.call-done = (f32[2,768,3,192]{1,3,2,0:T(8,128)}, f32[2,192,768]{2,1,0:T(8,128)}, f32[2,768,768]{2,1,0:T(8,128)}, f32[2,768,768]{2,1,0:T(8,128)}) async-done(((f32[2,768,3,192]{1,3,2,0:T(8,128)}, f32[2,192,768]{2,1,0:T(8,128)}, f32[2,768,768]{2,1,0:T(8,128)}, f32[2,768,768]{2,1,0:T(8,128)}), (f32[2,768,3,192]{1,3,2,0:T(8,128)}, f32[2,192,768]{2,1,0:T(8,128)}, f32[2,768,768]{2,1,0:T(8,128)}, ...) | async-done | bytes 14155792 | tf_op jit(solution)/shard_map/psum | solution.py:376
  (527 shorter events, 456.5 us)
Async XLA Ops:
  7.2 340.7 %copy-start = (s32[4,2]{0,1:T(2,128)S(1)}, s32[4,2]{0,1:T(2,128)}, u32[]{:S(2)}) copy-start(s32[4,2]{0,1:T(2,128)} %param.23) | copy-start | bytes 100
  7.2 151.5 %all-gather.9.cloned.1.call-start = ((), (), s32[]{:S(2)}) async-start(), calls=%async_computation.8 | async-start | bytes 1966080 | tf_op jit(solution)/shard_map/all_gather | solution.py:225
  13.2 190.5 %reduce-scatter.9.cloned.1.call-start = ((), (), s32[]{:S(2)}) async-start(), calls=%async_computation.9 | async-start | bytes 1966080 | tf_op jit(solution)/shard_map/reduce_scatter | solution.py:231
  15.4 128.6 %copy-start.102 = (s32[1024]{0:T(1024)S(1)}, s32[1024]{0:T(1024)}, u32[]{:S(2)}) copy-start(s32[1024]{0:T(1024)} %param.22) | copy-start | bytes 12292
  15.4 128.6 %copy-start.104 = (bf16[2,2,192]{2,1,0:T(2,128)(2,1)S(1)}, bf16[2,2,192]{2,1,0:T(2,128)(2,1)}, u32[]{:S(2)}) copy-start(bf16[2,2,192]{2,1,0:T(2,128)(2,1)} %param.26) | copy-start | bytes 4612
  144.8 20.2 %copy-start.91 = (f32[3,64]{1,0:T(4,128)}, f32[3,64]{1,0:T(4,128)S(1)}, u32[]{:S(2)}) copy-start(f32[3,64]{1,0:T(4,128)S(1)} %add.315) | copy-start | bytes 2308
  169.7 33.9 %copy-start.4 = (bf16[256,768]{1,0:T(8,128)(2,1)S(1)}, bf16[256,768]{1,0:T(8,128)(2,1)}, u32[]{:S(2)}) copy-start(bf16[256,768]{1,0:T(8,128)(2,1)} %param.20) | copy-start | bytes 1179652
  172.7 56.0 %all-gather.11.cloned.1.call-start = ((), (), s32[]{:S(2)}) async-start(), calls=%async_computation.10 | async-start | bytes 1966080 | tf_op jit(solution)/shard_map/all_gather | solution.py:225
  208.8 62.9 %reduce-scatter.11.cloned.1.call-start = ((), (), s32[]{:S(2)}) async-start(), calls=%async_computation.11 | async-start | bytes 1966080 | tf_op jit(solution)/shard_map/reduce_scatter | solution.py:231
  228.7 12.1 copy-start.106
  243.3 52.2 %all-gather.13.cloned.1.call-start = ((), (), s32[]{:S(2)}) async-start(), calls=%async_computation.12 | async-start | bytes 1966080 | tf_op jit(solution)/shard_map/all_gather | solution.py:225
  275.7 68.1 %reduce-scatter.13.cloned.1.call-start = ((), (), s32[]{:S(2)}) async-start(), calls=%async_computation.13 | async-start | bytes 1966080 | tf_op jit(solution)/shard_map/reduce_scatter | solution.py:231
  315.5 52.1 %all-gather.15.cloned.1.call-start = ((), (), s32[]{:S(2)}) async-start(), calls=%async_computation.14 | async-start | bytes 1966080 | tf_op jit(solution)/shard_map/all_gather | solution.py:225
  347.8 41.2 %all-gather.17.cloned.1.call-start = ((), (), s32[]{:S(2)}) async-start(), calls=%async_computation.16 | async-start | bytes 1966080 | tf_op jit(solution)/shard_map/all_gather | solution.py:228
  349.2 18.4 %copy-start.105 = (pred[256]{0:T(512)(128)(4,1)}, pred[256]{0:T(512)(128)(4,1)S(1)}, u32[]{:S(2)}) copy-start(pred[256]{0:T(512)(128)(4,1)S(1)} %dynamic_slice.14) | copy-start | bytes 772
  351.1 75.5 %reduce-scatter.17.cloned.1.call-start = ((), (), s32[]{:S(2)}) async-start(), calls=%async_computation.17 | async-start | bytes 1966080 | tf_op jit(solution)/shard_map/reduce_scatter | solution.py:239
  367.6 21.4 %copy-start.100 = (f32[768]{0:T(1024)S(1)}, f32[768]{0:T(1024)}, u32[]{:S(2)}) copy-start(f32[768]{0:T(1024)} %get-tuple-element.153) | copy-start | bytes 9220
  398.3 58.9 %reduce-scatter.15.cloned.1.call-start = ((), (), s32[]{:S(2)}) async-start(), calls=%async_computation.15 | async-start | bytes 1966080 | tf_op jit(solution)/shard_map/reduce_scatter | solution.py:231
  398.4 28.3 %copy-start.45 = (f32[768]{0:T(1024)S(1)}, f32[768]{0:T(1024)}, u32[]{:S(2)}) copy-start(f32[768]{0:T(1024)} %get-tuple-element.239) | copy-start | bytes 9220
  402.7 79.7 %all-gather.19.cloned.1.call-start = ((), (), s32[]{:S(2)}) async-start(), calls=%async_computation.18 | async-start | bytes 1966080 | tf_op jit(solution)/shard_map/all_gather | solution.py:228
  462.6 81.7 %reduce-scatter.19.cloned.1.call-start = ((), (), s32[]{:S(2)}) async-start(), calls=%async_computation.19 | async-start | bytes 1966080 | tf_op jit(solution)/shard_map/reduce_scatter | solution.py:239
  466.5 24.2 %copy-start.98 = (f32[3,64]{1,0:T(4,128)S(1)}, f32[3,64]{1,0:T(4,128)}, u32[]{:S(2)}) copy-start(f32[3,64]{1,0:T(4,128)} %add.339) | copy-start | bytes 2308
  512.2 32.1 %copy-start.44 = (f32[768]{0:T(1024)S(1)}, f32[768]{0:T(1024)}, u32[]{:S(2)}) copy-start(f32[768]{0:T(1024)} %get-tuple-element.236) | copy-start | bytes 9220
  516.0 54.8 %all-gather.21.cloned.1.call-start = ((), (), s32[]{:S(2)}) async-start(), calls=%async_computation.20 | async-start | bytes 1966080 | tf_op jit(solution)/shard_map/all_gather | solution.py:228
  551.0 57.4 %reduce-scatter.21.cloned.1.call-start = ((), (), s32[]{:S(2)}) async-start(), calls=%async_computation.21 | async-start | bytes 1966080 | tf_op jit(solution)/shard_map/reduce_scatter | solution.py:239
  580.1 54.5 %all-gather.23.cloned.1.call-start = ((), (), s32[]{:S(2)}) async-start(), calls=%async_computation.22 | async-start | bytes 1966080 | tf_op jit(solution)/shard_map/all_gather | solution.py:228
  614.8 240.3 %reduce-scatter.23.cloned.1.call-start = ((), (), s32[]{:S(2)}) async-start(), calls=%async_computation.23 | async-start | bytes 1966080 | tf_op jit(solution)/shard_map/reduce_scatter | solution.py:239
  653.3 286.6 %all-reduce.6.cloned.1.call-start = ((), (), s32[]{:S(2)}) async-start(), calls=%async_computation.24 | async-start | bytes 167936 | tf_op jit(solution)/shard_map/psum | solution.py:376
  668.3 179.1 %copy-start.95 = (f32[3,64]{1,0:T(4,128)S(1)}, f32[3,64]{1,0:T(4,128)}, u32[]{:S(2)}) copy-start(f32[3,64]{1,0:T(4,128)} %get-tuple-element.230) | copy-start | bytes 2308
  668.3 180.7 %copy-start.94 = (f32[1,2,192]{2,1,0:T(2,128)S(1)}, f32[1,2,192]{2,1,0:T(2,128)}, u32[]{:S(2)}) copy-start(f32[1,2,192]{2,1,0:T(2,128)} %maximum_bitcast_fusion.10) | copy-start | bytes 4612
  854.6 13.5 copy-start.26
  868.0 517.2 %all-reduce.8.cloned.1.call-start = ((), (), s32[]{:S(2)}) async-start(), calls=%async_computation.25 | async-start | bytes 28311552 | tf_op jit(solution)/shard_map/psum | solution.py:376
  (106 other events, 296.6 us)
Sparse Core Ops, SparseCore 0:
  13.3 22.3 all-gather.8
  172.8 30.8 reduce-scatter.8
  208.9 19.6 all-gather.10
  243.5 28.1 reduce-scatter.10
  275.8 19.6 all-gather.12
  315.6 28.1 reduce-scatter.12
  347.9 19.6 all-gather.14
  369.2 19.7 all-gather.16
  398.4 28.1 reduce-scatter.16
  429.0 28.1 reduce-scatter.14
  462.7 19.6 all-gather.18
  516.1 28.1 reduce-scatter.18
  551.1 19.6 all-gather.20
  580.2 28.1 reduce-scatter.20
  614.9 19.6 all-gather.22
  653.4 28.1 reduce-scatter.22
  868.2 71.7 all-reduce.5
  945.0 440.1 all-reduce.7
